TPU v7x, 128 devices: a whole 4x4x4 slice. The times are simulated.
128 devices in a mesh: ctx: 32 (over y, z, core), tp: 4 (over x).
Axes of the slice: x: 4, y: 4, z: 4, core: 2. Of those that a mesh axis runs over, the one named last changes fastest.
Arguments:
- query: bfloat16 [16384, 6144], P('ctx', 'tp'), may hold values from -6 to 6
- key_in: bfloat16 [16384, 6144], P('ctx', 'tp'), may hold values from -6 to 6
- value_in: bfloat16 [16384, 6144], P('ctx', 'tp'), may hold values from -6 to 6
- dout: bfloat16 [16384, 6144], P('ctx', 'tp'), may hold values from -0.5 to 0.5
- summary_offset: int32 [4], replicated, may hold values from 0 to 31
Outputs:
- grad_query: bfloat16 [16384, 6144], P(('ctx', 'tp'))
- grad_key: bfloat16 [16384, 6144], P(('ctx', 'tp'))
- grad_value: bfloat16 [16384, 6144], P(('ctx', 'tp'))
Inputs may be any that keep to these rules, and one draw needn't show every extreme that they name: Summary block s is block s * 32 + summary_offset[s].
All inputs are finite; a program needn't handle non-finite values.
Results may differ from a plain program's by a relative error of at most 0.014.
Values may be sent and summed in bfloat16 or wider, within the bound.
No kernel may reach another device: no remote copies, remote signals or barrier semaphores. Data moves between devices by JAX's collectives and lax.ppermute only.
A program may use at most 128 MiB of HBM per device.

v0:
```python
import jax
import jax.numpy as jnp
from jax import lax
from jax.sharding import PartitionSpec as P

HDIM = 128
BLOCK = 128
BAND = 8
STRIDE = 32
REACH = 2


def passed_along(value, axis, steps):
    count = lax.axis_size(axis)
    leading, last = (max(0, -steps), min(count, count - steps))
    return lax.ppermute(value, axis, [(source, source + steps) for source in range(leading, last)])


def broadcast(value, axis, source):
    kept = jnp.where(lax.axis_index(axis) == source, value, 0).astype(value.dtype)
    return lax.psum(kept, axis)


def band_mask(query_tok, key_tok):
    return (
        (key_tok >= 0)
        & (key_tok <= query_tok)
        & (key_tok // BLOCK >= query_tok // BLOCK - (BAND - 1))
    )


def column(array, start):
    return lax.dynamic_slice_in_dim(array, start, HDIM, 1)


def in_summary(tokens, groups):
    return jnp.any((tokens // BLOCK)[:, None] == groups[None, :], axis=1)


def on_device(query, key_in, value_in, dout, summary_offset):
    rows, width = query.shape
    heads_here = width // HDIM
    me = lax.axis_index("ctx")
    n_ctx = lax.axis_size("ctx")
    scale = HDIM ** (-0.5)
    n_sum = summary_offset.shape[0]
    groups = jnp.arange(n_sum, dtype=jnp.int32) * STRIDE + summary_offset
    owner = groups * BLOCK // rows
    local_start = groups * BLOCK - owner * rows
    within = jnp.arange(BLOCK, dtype=jnp.int32)
    tile_rows = (local_start[:, None] + within[None, :]).reshape(-1)
    sum_tok = (groups[:, None] * BLOCK + within[None, :]).reshape(-1)
    sum_owner = jnp.repeat(owner, BLOCK)
    mine = (sum_owner == me)[:, None]

    def fetch(distance):
        return passed_along((key_in, value_in), "ctx", distance)

    fetched = [fetch(distance) for distance in range(REACH, 0, -1)]
    ext_k = jnp.concatenate([piece[0] for piece in fetched] + [key_in], axis=0)
    ext_v = jnp.concatenate([piece[1] for piece in fetched] + [value_in], axis=0)

    def fill(index, carry):
        start = local_start[index]
        tile = (
            lax.dynamic_slice_in_dim(key_in, start, BLOCK, 0),
            lax.dynamic_slice_in_dim(value_in, start, BLOCK, 0),
        )
        got_k, got_v = (
            broadcast(tile[0], "ctx", owner[index]),
            broadcast(tile[1], "ctx", owner[index]),
        )
        return (
            lax.dynamic_update_slice_in_dim(carry[0], got_k, index * BLOCK, 0),
            lax.dynamic_update_slice_in_dim(carry[1], got_v, index * BLOCK, 0),
        )

    empty = jnp.zeros((n_sum * BLOCK, width), jnp.bfloat16)
    sum_k, sum_v = lax.fori_loop(0, n_sum, fill, (empty, empty))
    key_all = jnp.concatenate([ext_k, sum_k], axis=0)
    value_all = jnp.concatenate([ext_v, sum_v], axis=0)
    query_tok = me * rows + jnp.arange(rows, dtype=jnp.int32)
    ext_tok = (me - REACH) * rows + jnp.arange((REACH + 1) * rows, dtype=jnp.int32)
    elsewhere = in_summary(ext_tok, groups) & (ext_tok < me * rows)
    band_part = (
        band_mask(query_tok[:, None], ext_tok[None, :]) & jnp.logical_not(elsewhere)[None, :]
    )
    sum_block = (sum_tok // BLOCK)[None, :]
    query_block = (query_tok // BLOCK)[:, None]
    before_band = sum_block < query_block - (BAND - 1)
    inside_band = (
        (sum_block >= query_block - (BAND - 1))
        & (sum_block <= query_block)
        & (sum_owner != me)[None, :]
    )
    summary_ok = before_band | inside_band
    allowed = jnp.concatenate([band_part, summary_ok], axis=1)
    first_key = REACH * rows
    kept = key_all.shape[0] - first_key

    def own_head(head, carry):
        grad_q, grad_k, grad_v, lse_all, delta_all = carry
        start = head * HDIM
        rows_q = column(query, start)
        rows_do = column(dout, start)
        keys = column(key_all, start)
        values = column(value_all, start)
        scores = jnp.einsum("qd,kd->qk", rows_q, keys, preferred_element_type=jnp.float32) * scale
        top = jnp.max(jnp.where(allowed, scores, -jnp.inf), axis=1, keepdims=True)
        total = jnp.sum(jnp.where(allowed, jnp.exp(scores - top), 0.0), axis=1, keepdims=True)
        lse = top + jnp.log(total)
        prob = jnp.where(allowed, jnp.exp(scores - lse), 0.0)
        dprob = jnp.einsum("qd,kd->qk", rows_do, values, preferred_element_type=jnp.float32)
        delta = jnp.sum(prob * dprob, axis=1, keepdims=True)
        dscore = (prob * (dprob - delta)).astype(jnp.bfloat16)
        prob_low = prob.astype(jnp.bfloat16)
        head_q = (
            jnp.einsum("qk,kd->qd", dscore, keys, preferred_element_type=jnp.float32) * scale
        ).astype(jnp.bfloat16)
        head_k = (
            jnp.einsum(
                "qk,qd->kd", dscore[:, first_key:], rows_q, preferred_element_type=jnp.float32
            )
            * scale
        )
        head_v = jnp.einsum(
            "qk,qd->kd", prob_low[:, first_key:], rows_do, preferred_element_type=jnp.float32
        )
        grad_q = lax.dynamic_update_slice_in_dim(grad_q, head_q, start, 1)
        grad_k = lax.dynamic_update_slice_in_dim(grad_k, head_k, start, 1)
        grad_v = lax.dynamic_update_slice_in_dim(grad_v, head_v, start, 1)
        lse_all = lax.dynamic_update_slice_in_dim(lse_all, lse.reshape(1, rows), head, 0)
        delta_all = lax.dynamic_update_slice_in_dim(delta_all, delta.reshape(1, rows), head, 0)
        return (grad_q, grad_k, grad_v, lse_all, delta_all)

    start_carry = (
        jnp.zeros((rows, width), jnp.bfloat16),
        jnp.zeros((kept, width), jnp.float32),
        jnp.zeros((kept, width), jnp.float32),
        jnp.zeros((heads_here, rows), jnp.float32),
        jnp.zeros((heads_here, rows), jnp.float32),
    )
    grad_q, grad_k, grad_v, lse_all, delta_all = lax.fori_loop(0, heads_here, own_head, start_carry)

    def remote_terms(later_q, later_do, later_lse, later_delta, later_mask):

        def remote_head(head, carry):
            acc_k, acc_v = carry
            start = head * HDIM
            rows_q = column(later_q, start)
            rows_do = column(later_do, start)
            keys = column(key_in, start)
            values = column(value_in, start)
            lse = lax.dynamic_slice_in_dim(later_lse, head, 1, 0).reshape(rows, 1)
            delta = lax.dynamic_slice_in_dim(later_delta, head, 1, 0).reshape(rows, 1)
            scores = (
                jnp.einsum("qd,kd->qk", rows_q, keys, preferred_element_type=jnp.float32) * scale
            )
            prob = jnp.where(later_mask, jnp.exp(scores - lse), 0.0)
            dprob = jnp.einsum("qd,kd->qk", rows_do, values, preferred_element_type=jnp.float32)
            dscore = (prob * (dprob - delta)).astype(jnp.bfloat16)
            prob_low = prob.astype(jnp.bfloat16)
            head_k = (
                jnp.einsum("qk,qd->kd", dscore, rows_q, preferred_element_type=jnp.float32) * scale
            )
            head_v = jnp.einsum("qk,qd->kd", prob_low, rows_do, preferred_element_type=jnp.float32)
            acc_k = lax.dynamic_update_slice_in_dim(acc_k, column(acc_k, start) + head_k, start, 1)
            acc_v = lax.dynamic_update_slice_in_dim(acc_v, column(acc_v, start) + head_v, start, 1)
            return (acc_k, acc_v)

        return remote_head

    local_k = grad_k[:rows]
    local_v = grad_v[:rows]
    local_tok = me * rows + jnp.arange(rows, dtype=jnp.int32)
    local_plain = jnp.logical_not(in_summary(local_tok, groups))[None, :]
    for distance in range(1, REACH + 1):
        inputs = passed_along((query, dout), "ctx", -distance)
        stats = passed_along((lse_all, delta_all), "ctx", -distance)
        (later_q, later_do), (later_lse, later_delta) = (inputs, stats)
        later_tok = (me + distance) * rows + jnp.arange(rows, dtype=jnp.int32)
        later_mask = (
            band_mask(later_tok[:, None], local_tok[None, :])
            & (later_tok < n_ctx * rows)[:, None]
            & local_plain
        )
        local_k, local_v = lax.fori_loop(
            0,
            heads_here,
            remote_terms(later_q, later_do, later_lse, later_delta, later_mask),
            (local_k, local_v),
        )
    summary_k = grad_k[rows:]
    summary_v = grad_v[rows:]
    total_k, total_v = lax.psum((summary_k, summary_v), "ctx")
    local_k = local_k.at[tile_rows].add(jnp.where(mine, total_k, 0.0))
    local_v = local_v.at[tile_rows].add(jnp.where(mine, total_v, 0.0))
    moved = (
        lax.all_to_all(grad_q, "tp", split_axis=0, concat_axis=1, tiled=True),
        lax.all_to_all(local_k.astype(jnp.bfloat16), "tp", split_axis=0, concat_axis=1, tiled=True),
        lax.all_to_all(local_v.astype(jnp.bfloat16), "tp", split_axis=0, concat_axis=1, tiled=True),
    )
    return (moved[0], moved[1], moved[2])


def solution(mesh):
    return jax.shard_map(
        on_device,
        mesh=mesh,
        in_specs=(P("ctx", "tp"), P("ctx", "tp"), P("ctx", "tp"), P("ctx", "tp"), P()),
        out_specs=(P(("ctx", "tp"), None), P(("ctx", "tp"), None), P(("ctx", "tp"), None)),
        check_vma=False,
    )
```

profile of v0, /device:TPU:8, one launch (start us, length us, event | category | flops | bytes accessed | tf_op | source)
XLA Modules:
  0.0 977.3 jit_solution(13444294860501639880)
XLA Ops:
  8.0 3.8 collective-permute-start
  13.8 3.8 collective-permute-start.2
  21.0 4.3 collective-permute-start.6
  28.9 20.7 %collective-permute-done = bf16[512,1536]{1,0:T(8,128)(2,1)} collective-permute-done((bf16[512,1536]{1,0:T(8,128)(2,1)}, bf16[512,1536]{1,0:T(8,128)(2,1)}, u32[]{:S(2)}, u32[]{:S(2)}) %collective-permute-start) | collective-permute-done | bytes 1572896 | tf_op jit(solution)/shard_map/ppermute | solution.py:16
  49.6 3.7 collective-permute-start.10
  53.3 27.9 %collective-permute-done.1 = bf16[512,1536]{1,0:T(8,128)(2,1)} collective-permute-done((bf16[512,1536]{1,0:T(8,128)(2,1)}, bf16[512,1536]{1,0:T(8,128)(2,1)}, u32[]{:S(2)}, u32[]{:S(2)}) %collective-permute-start.1) | collective-permute-done | bytes 1572896 | tf_op jit(solution)/shard_map/ppermute | solution.py:16
  85.6 458.6 %while.70 = (s32[]{:T(128)}, bf16[512,1536]{1,0:T(8,128)(2,1)}, bf16[512,1536]{1,0:T(8,128)(2,1)}, s32[4]{0:T(128)S(1)}, s32[4]{0:T(128)S(1)}, /*index=5*/bf16[5...) while((s32[]{:T(128)}, bf16[512,1536]{1,0:T(8,128)(2,1)}, ...), condition=%wide.region_3.4_spmd, body=%wide.region_0.3_spmd.sunk | while | flops 786445 | bytes 7864643 | solution.py:79
  91.5 108.0 %all-reduce.9.cloned.1.call-done = (bf16[128,1536]{1,0:T(8,128)(2,1)}, bf16[128,1536]{1,0:T(8,128)(2,1)}) async-done(((bf16[128,1536]{1,0:T(8,128)(2,1)}, bf16[128,1536]{1,0:T(8,128)(2,1)}), (bf16[128,1536]{1,0:T(8,128)(2,1)}, bf16[128,1536]{1,0:T(8,128)(2,1)})) %all-reduce.9.cloned.1.call-update) | async-done | bytes 786448 | tf_op jit(solution)/shard_map/while/body/eval_jaxpr/psum | solution.py:21
  208.9 104.3 %all-reduce.9.cloned.1.call-done = (bf16[128,1536]{1,0:T(8,128)(2,1)}, bf16[128,1536]{1,0:T(8,128)(2,1)}) async-done(((bf16[128,1536]{1,0:T(8,128)(2,1)}, bf16[128,1536]{1,0:T(8,128)(2,1)}), (bf16[128,1536]{1,0:T(8,128)(2,1)}, bf16[128,1536]{1,0:T(8,128)(2,1)})) %all-reduce.9.cloned.1.call-update) | async-done | bytes 786448 | tf_op jit(solution)/shard_map/while/body/eval_jaxpr/psum | solution.py:21
  322.6 104.3 %all-reduce.9.cloned.1.call-done = (bf16[128,1536]{1,0:T(8,128)(2,1)}, bf16[128,1536]{1,0:T(8,128)(2,1)}) async-done(((bf16[128,1536]{1,0:T(8,128)(2,1)}, bf16[128,1536]{1,0:T(8,128)(2,1)}), (bf16[128,1536]{1,0:T(8,128)(2,1)}, bf16[128,1536]{1,0:T(8,128)(2,1)})) %all-reduce.9.cloned.1.call-update) | async-done | bytes 786448 | tf_op jit(solution)/shard_map/while/body/eval_jaxpr/psum | solution.py:21
  436.3 104.3 %all-reduce.9.cloned.1.call-done = (bf16[128,1536]{1,0:T(8,128)(2,1)}, bf16[128,1536]{1,0:T(8,128)(2,1)}) async-done(((bf16[128,1536]{1,0:T(8,128)(2,1)}, bf16[128,1536]{1,0:T(8,128)(2,1)}), (bf16[128,1536]{1,0:T(8,128)(2,1)}, bf16[128,1536]{1,0:T(8,128)(2,1)})) %all-reduce.9.cloned.1.call-update) | async-done | bytes 786448 | tf_op jit(solution)/shard_map/while/body/eval_jaxpr/psum | solution.py:21
  544.2 6.5 pad_maximum_fusion
  550.7 4.9 pad_maximum_fusion.1
  563.6 162.5 %while.71 = (s32[]{:T(128)}, bf16[512,1536]{1,0:T(8,128)(2,1)}, f32[1024,1536]{1,0:T(8,128)}, f32[1024,1536]{1,0:T(8,128)}, f32[12,512]{1,0:T(8,128)S(1)}, /*ind...) while((s32[]{:T(128)}, bf16[512,1536]{1,0:T(8,128)(2,1)}, ...), condition=%wide.region_9.10_spmd, body=%wide.region_5.9_spmd.sunk | while | flops 1089731584 | bytes 42106048 | solution.py:143
  726.1 4.3 collective-permute-start.5
  733.5 6.2 fusion.102
  742.8 4.4 all-to-all-start
  755.6 75.6 %while.72 = (s32[]{:T(128)}, f32[512,1536]{1,0:T(8,128)}, f32[512,1536]{1,0:T(8,128)}, bf16[512,1536]{1,0:T(8,128)(2,1)}, bf16[512,1536]{1,0:T(8,128)(2,1)}, /*i...) while((s32[]{:T(128)}, f32[512,1536]{1,0:T(8,128)}, ...), condition=%wide.region_12.13_spmd.clone, body=%wide.region_11.12_spmd.clone.sunk | while | flops 272039936 | bytes 5007079 | solution.py:187
  831.2 75.5 %while.73 = (s32[]{:T(128)}, f32[512,1536]{1,0:T(8,128)}, f32[512,1536]{1,0:T(8,128)}, bf16[512,1536]{1,0:T(8,128)(2,1)}, bf16[512,1536]{1,0:T(8,128)(2,1)}, /*i...) while((s32[]{:T(128)}, f32[512,1536]{1,0:T(8,128)}, ...), condition=%wide.region_14.15_spmd.clone, body=%wide.region_13.14_spmd.clone.sunk | while | flops 272039936 | bytes 5007079 | solution.py:187
  906.7 10.6 %scatter_custom_fusion.1 = f32[512,1536]{1,0:T(8,128)} fusion(f32[512,1536]{1,0:T(8,128)} %get-tuple-element.718, s32[512]{0:T(512)S(1)} %bitcast.76, f32[512,1536]{1,0:T(8,128)} %get-tuple-element.910, f32[]{:T(128)} %constant.333.clone.1, pred[512]{0:T(512)(128)(4,1)S(1)} %broadcast_bitcast_fusion), kind=kCustom, calls=%fused_computation.91 | custom fusion | flops 1572864 | bytes 6292480 | tf_op jit(solution)/shard_map/scatter-add | solution.py:197
  920.7 4.7 all-to-all-start.2
  925.4 8.2 scatter_custom_fusion
  935.0 10.3 %all-to-all-done.2 = bf16[4,128,1536]{2,1,0:T(8,128)(2,1)} async-done(((bf16[4,128,1536]{2,1,0:T(8,128)(2,1)}), bf16[4,128,1536]{2,1,0:T(8,128)(2,1)}, u32[]{:S(2)}, u32[]{:S(2)}) %all-to-all-start.2) | async-done | bytes 1572896 | tf_op jit(solution)/shard_map/all_to_all | solution.py:201
  955.8 11.9 %all-to-all-done.1 = bf16[4,128,1536]{2,1,0:T(8,128)(2,1)S(1)} async-done(((bf16[4,128,1536]{2,1,0:T(8,128)(2,1)}), bf16[4,128,1536]{2,1,0:T(8,128)(2,1)S(1)}, u32[]{:S(2)}, u32[]{:S(2)}) %all-to-all-start.1) | async-done | bytes 1572896 | tf_op jit(solution)/shard_map/all_to_all | solution.py:200
  (313 shorter events, 393.7 us)
Async XLA Ops:
  8.0 41.6 %collective-permute-start = (bf16[512,1536]{1,0:T(8,128)(2,1)}, bf16[512,1536]{1,0:T(8,128)(2,1)}, u32[]{:S(2)}, u32[]{:S(2)}) collective-permute-start(bf16[512,1536]{1,0:T(8,128)(2,1)} %param.14), channel_id=1, source_target_pairs={{0,8},{4,12},{8,16},{12,20},{16,24},{20,28},{24,32},{28,36},{32,40... | collective-permute-start | bytes 4718600 | tf_op jit(solution)/shard_map/ppermute | solution.py:16
  11.8 69.3 %collective-permute-start.1 = (bf16[512,1536]{1,0:T(8,128)(2,1)}, bf16[512,1536]{1,0:T(8,128)(2,1)}, u32[]{:S(2)}, u32[]{:S(2)}) collective-permute-start(bf16[512,1536]{1,0:T(8,128)(2,1)} %param.14), channel_id=1, source_target_pairs={{0,4},{4,8},{8,12},{12,16},{16,20},{20,24},{24,28},{28,32},{32,36}... | collective-permute-start | bytes 4718600 | tf_op jit(solution)/shard_map/ppermute | solution.py:16
  13.8 536.9 %collective-permute-start.2 = (bf16[512,1536]{1,0:T(8,128)(2,1)}, bf16[512,1536]{1,0:T(8,128)(2,1)}, u32[]{:S(2)}, u32[]{:S(2)}) collective-permute-start(bf16[512,1536]{1,0:T(8,128)(2,1)} %param.15), channel_id=1, source_target_pairs={{0,8},{4,12},{8,16},{12,20},{16,24},{20,28},{24,32},{28,36},{32,40... | collective-permute-start | bytes 4718600 | tf_op jit(solution)/shard_map/ppermute | solution.py:16
  17.6 533.0 %collective-permute-start.3 = (bf16[512,1536]{1,0:T(8,128)(2,1)}, bf16[512,1536]{1,0:T(8,128)(2,1)}, u32[]{:S(2)}, u32[]{:S(2)}) collective-permute-start(bf16[512,1536]{1,0:T(8,128)(2,1)} %param.15), channel_id=1, source_target_pairs={{0,4},{4,8},{8,12},{12,16},{16,20},{20,24},{24,28},{28,32},{32,36}... | collective-permute-start | bytes 4718600 | tf_op jit(solution)/shard_map/ppermute | solution.py:16
  21.0 728.7 %collective-permute-start.6 = (bf16[512,1536]{1,0:T(8,128)(2,1)}, bf16[512,1536]{1,0:T(8,128)(2,1)}, u32[]{:S(2)}, u32[]{:S(2)}) collective-permute-start(bf16[512,1536]{1,0:T(8,128)(2,1)} %param.16), channel_id=1, source_target_pairs={{4,0},{8,4},{12,8},{16,12},{20,16},{24,20},{28,24},{32,28},{36,32}... | collective-permute-start | bytes 4718600 | tf_op jit(solution)/shard_map/ppermute | solution.py:16
  27.3 58.3 %copy-start.2 = (bf16[512,1536]{1,0:T(8,128)(2,1)S(1)}, bf16[512,1536]{1,0:T(8,128)(2,1)}, u32[]{:S(2)}) copy-start(bf16[512,1536]{1,0:T(8,128)(2,1)} %param.15) | copy-start | bytes 4718596
  49.6 781.6 %collective-permute-start.10 = (bf16[512,1536]{1,0:T(8,128)(2,1)}, bf16[512,1536]{1,0:T(8,128)(2,1)}, u32[]{:S(2)}, u32[]{:S(2)}) collective-permute-start(bf16[512,1536]{1,0:T(8,128)(2,1)} %param.16), channel_id=1, source_target_pairs={{8,0},{12,4},{16,8},{20,12},{24,16},{28,20},{32,24},{36,28},{40,32... | collective-permute-start | bytes 4718600 | tf_op jit(solution)/shard_map/ppermute | solution.py:16
  81.2 666.6 %collective-permute-start.4 = (bf16[512,1536]{1,0:T(8,128)(2,1)}, bf16[512,1536]{1,0:T(8,128)(2,1)}, u32[]{:S(2)}, u32[]{:S(2)}) collective-permute-start(bf16[512,1536]{1,0:T(8,128)(2,1)} %param.13), channel_id=1, source_target_pairs={{4,0},{8,4},{12,8},{16,12},{20,16},{24,20},{28,24},{32,28},{36,32}... | collective-permute-start | bytes 4718600 | tf_op jit(solution)/shard_map/ppermute | solution.py:16
  85.6 113.9 %all-reduce.9.cloned.1.call-start = ((), (), s32[]{:S(2)}) async-start(), calls=%async_computation.4 | async-start | bytes 1572864 | tf_op jit(solution)/shard_map/while/body/eval_jaxpr/psum | solution.py:21
  203.0 110.2 %all-reduce.9.cloned.1.call-start = ((), (), s32[]{:S(2)}) async-start(), calls=%async_computation.4 | async-start | bytes 1572864 | tf_op jit(solution)/shard_map/while/body/eval_jaxpr/psum | solution.py:21
  316.7 110.2 %all-reduce.9.cloned.1.call-start = ((), (), s32[]{:S(2)}) async-start(), calls=%async_computation.4 | async-start | bytes 1572864 | tf_op jit(solution)/shard_map/while/body/eval_jaxpr/psum | solution.py:21
  430.5 110.2 %all-reduce.9.cloned.1.call-start = ((), (), s32[]{:S(2)}) async-start(), calls=%async_computation.4 | async-start | bytes 1572864 | tf_op jit(solution)/shard_map/while/body/eval_jaxpr/psum | solution.py:21
  544.2 6.5 copy-start.3
  726.1 26.0 %collective-permute-start.5 = (f32[12,512]{1,0:T(8,128)S(1)}, f32[12,512]{1,0:T(8,128)S(1)}, u32[]{:S(2)}, u32[]{:S(2)}) collective-permute-start(f32[12,512]{1,0:T(8,128)S(1)} %get-tuple-element.713), channel_id=1, source_target_pairs={{4,0},{8,4},{12,8},{16,12},{20,16},{24,20},{28,24},{32,28},{36,32}... | collective-permute-start | bytes 73736 | tf_op jit(solution)/shard_map/ppermute | solution.py:16
  730.4 25.2 %collective-permute-start.7 = (f32[12,512]{1,0:T(8,128)S(1)}, f32[12,512]{1,0:T(8,128)S(1)}, u32[]{:S(2)}, u32[]{:S(2)}) collective-permute-start(f32[12,512]{1,0:T(8,128)S(1)} %get-tuple-element.714), channel_id=1, source_target_pairs={{4,0},{8,4},{12,8},{16,12},{20,16},{24,20},{28,24},{32,28},{36,32}... | collective-permute-start | bytes 73736 | tf_op jit(solution)/shard_map/ppermute | solution.py:16
  733.4 6.3 copy-start.1
  742.8 177.9 %all-to-all-start = ((bf16[4,128,1536]{2,1,0:T(8,128)(2,1)}), bf16[4,128,1536]{2,1,0:T(8,128)(2,1)}, u32[]{:S(2)}, u32[]{:S(2)}) async-start(bf16[4,128,1536]{2,1,0:T(8,128)(2,1)} %bitcast.63), calls=%async_computation | async-start | bytes 3145728 | tf_op jit(solution)/shard_map/all_to_all | solution.py:199
  747.2 159.6 %all-reduce.7.cloned.1.call-start = ((), (), s32[]{:S(2)}) async-start(), calls=%async_computation.3 | async-start | bytes 12582912 | tf_op jit(solution)/shard_map/psum | solution.py:195
  747.8 83.4 %collective-permute-start.8 = (bf16[512,1536]{1,0:T(8,128)(2,1)}, bf16[512,1536]{1,0:T(8,128)(2,1)}, u32[]{:S(2)}, u32[]{:S(2)}) collective-permute-start(bf16[512,1536]{1,0:T(8,128)(2,1)} %param.13), channel_id=1, source_target_pairs={{8,0},{12,4},{16,8},{20,12},{24,16},{28,20},{32,24},{36,28},{40,32... | collective-permute-start | bytes 4718600 | tf_op jit(solution)/shard_map/ppermute | solution.py:16
  749.7 81.5 %collective-permute-start.11 = (f32[12,512]{1,0:T(8,128)S(1)}, f32[12,512]{1,0:T(8,128)S(1)}, u32[]{:S(2)}, u32[]{:S(2)}) collective-permute-start(f32[12,512]{1,0:T(8,128)S(1)} %get-tuple-element.714), channel_id=1, source_target_pairs={{8,0},{12,4},{16,8},{20,12},{24,16},{28,20},{32,24},{36,28},{40,32... | collective-permute-start | bytes 73736 | tf_op jit(solution)/shard_map/ppermute | solution.py:16
  752.1 79.1 %collective-permute-start.9 = (f32[12,512]{1,0:T(8,128)S(1)}, f32[12,512]{1,0:T(8,128)S(1)}, u32[]{:S(2)}, u32[]{:S(2)}) collective-permute-start(f32[12,512]{1,0:T(8,128)S(1)} %get-tuple-element.713), channel_id=1, source_target_pairs={{8,0},{12,4},{16,8},{20,12},{24,16},{28,20},{32,24},{36,28},{40,32... | collective-permute-start | bytes 73736 | tf_op jit(solution)/shard_map/ppermute | solution.py:16
  917.4 8.1 copy-start
  920.7 24.6 %all-to-all-start.2 = ((bf16[4,128,1536]{2,1,0:T(8,128)(2,1)}), bf16[4,128,1536]{2,1,0:T(8,128)(2,1)}, u32[]{:S(2)}, u32[]{:S(2)}) async-start(bf16[4,128,1536]{2,1,0:T(8,128)(2,1)} %bitcast.67), calls=%async_computation.2 | async-start | bytes 3145728 | tf_op jit(solution)/shard_map/all_to_all | solution.py:201
  945.3 22.4 %all-to-all-start.1 = ((bf16[4,128,1536]{2,1,0:T(8,128)(2,1)}), bf16[4,128,1536]{2,1,0:T(8,128)(2,1)S(1)}, u32[]{:S(2)}, u32[]{:S(2)}) async-start(bf16[4,128,1536]{2,1,0:T(8,128)(2,1)} %bitcast.68), calls=%async_computation.1 | async-start | bytes 3145728 | tf_op jit(solution)/shard_map/all_to_all | solution.py:200
Sparse Core Ops, SparseCore 0:
  91.6 107.8 all-reduce.8
  209.0 104.1 all-reduce.8
  322.7 104.1 all-reduce.8
  436.5 104.1 all-reduce.8
Sparse Core Ops, SparseCore 1:
  751.2 130.4 all-reduce.6
where the time goes:
time: 982 us; the launch traced here: 977 us
  waiting for transfers between devices  492 us (50%)
  matrix products  291 us (30%)
  other arithmetic  66.8 us (7%)
  starting transfers between devices  50.7 us (5%)
  local copies, waits for them, and re-layouts  49.6 us (5%)
  between operations  15.5 us (2%)
  loops' own time  11.1 us (1%)
    psum x4, waiting for transfers between devices, broadcast(): return lax.psum(kept, axis)  421 us
    dot_general x24, matrix products, remote_head(): jnp.einsum('qk,qd->kd', dscore, rows_q, preferred_element_type=jnp.float32)  61.8 us
    dot_general x24, matrix products, remote_head(): jnp.einsum('qk,qd->kd', prob_low, rows_do, preferred_element_type=jnp.flo...  50.9 us
    ppermute x12, waiting for transfers between devices, passed_along(): lax.ppermute(value, axis, [(source, source + steps) for source in range(l...  48.6 us
    ppermute x12, starting transfers between devices, passed_along(): lax.ppermute(value, axis, [(source, source + steps) for source in range(l...  38 us
    dot_general x24, matrix products, remote_head(): jnp.einsum('qd,kd->qk', rows_q, keys, preferred_element_type=jnp.float32)  37.9 us
    dot_general x12, matrix products, own_head(): jnp.einsum('qd,kd->qk', rows_do, values, preferred_element_type=jnp.float32)  32.6 us
    dot_general x12, matrix products, own_head(): jnp.einsum('qk,kd->qd', dscore, keys, preferred_element_type=jnp.float32)  28.9 us
  transfers between devices with their start and end apart: 20, of which 8 were waited for; matrix products, arithmetic and copies ran while one was open for 41% of the time, Pallas kernels for 0%

commit v1 on v0

--- a/solution.py
+++ b/solution.py
@@ -18,7 +18,7 @@
 
 def broadcast(value, axis, source):
     kept = jnp.where(lax.axis_index(axis) == source, value, 0).astype(value.dtype)
-    return lax.psum(kept, axis)
+    return jnp.sum(lax.all_gather(kept, axis), axis=0)
 
 
 def band_mask(query_tok, key_tok):

time: 982 us -> 1090 us (1.11)
  waiting for transfers between devices: 492 us -> 556 us
  other arithmetic: 66.8 us -> 122 us
    all_gather x0 -> x8, waiting for transfers between devices: none -> 484 us  [broadcast(): return jnp.sum(lax.all_gather(kept, axis), axis=0)]
    psum x4 -> x0, waiting for transfers between devices: 421 us -> none  [broadcast(): return lax.psum(kept, axis)]
    reduce_sum x0 -> x8, other arithmetic: none -> 52.9 us  [broadcast(): return jnp.sum(lax.all_gather(kept, axis), axis=0)]
  transfers between devices with their start and end apart: 20 -> 24, of which waited for: 8 -> 12; matrix products, arithmetic and copies ran while one was open for 41% -> 42% of each run, Pallas kernels for 0% -> 0%
where the time goes in v1:
time: 1090 us
  waiting for transfers between devices  556 us (51%)
  matrix products  291 us (27%)
  other arithmetic  122 us (11%)
  starting transfers between devices  50.3 us (5%)
  local copies, waits for them, and re-layouts  41.7 us (4%)
  between operations  15.8 us (1%)
  loops' own time  11.1 us (1%)
    all_gather x8, waiting for transfers between devices, broadcast(): return jnp.sum(lax.all_gather(kept, axis), axis=0)  484 us
    dot_general x24, matrix products, remote_head(): jnp.einsum('qk,qd->kd', dscore, rows_q, preferred_element_type=jnp.float32)  61.8 us
    reduce_sum x8, other arithmetic, broadcast(): return jnp.sum(lax.all_gather(kept, axis), axis=0)  52.9 us
    dot_general x24, matrix products, remote_head(): jnp.einsum('qk,qd->kd', prob_low, rows_do, preferred_element_type=jnp.flo...  50.9 us
    ppermute x12, waiting for transfers between devices, passed_along(): lax.ppermute(value, axis, [(source, source + steps) for source in range(l...  48.6 us
    dot_general x24, matrix products, remote_head(): jnp.einsum('qd,kd->qk', rows_q, keys, preferred_element_type=jnp.float32)  37.9 us
    ppermute x12, starting transfers between devices, passed_along(): lax.ppermute(value, axis, [(source, source + steps) for source in range(l...  37.6 us
    dot_general x12, matrix products, own_head(): jnp.einsum('qd,kd->qk', rows_do, values, preferred_element_type=jnp.float32)  32.6 us
  transfers between devices with their start and end apart: 24, of which 12 were waited for; matrix products, arithmetic and copies ran while one was open for 42% of the time, Pallas kernels for 0%

profile of v1, /device:TPU:8, one launch (start us, length us, event | category | flops | bytes accessed | tf_op | source)
XLA Modules:
  0.0 1088.8 jit_solution(7967635833759064092)
XLA Ops:
  28.9 20.7 %collective-permute-done = bf16[512,1536]{1,0:T(8,128)(2,1)} collective-permute-done((bf16[512,1536]{1,0:T(8,128)(2,1)}, bf16[512,1536]{1,0:T(8,128)(2,1)}, u32[]{:S(2)}, u32[]{:S(2)}) %collective-permute-start) | collective-permute-done | bytes 1572896 | tf_op jit(solution)/shard_map/ppermute | solution.py:16
  53.3 27.9 %collective-permute-done.1 = bf16[512,1536]{1,0:T(8,128)(2,1)} collective-permute-done((bf16[512,1536]{1,0:T(8,128)(2,1)}, bf16[512,1536]{1,0:T(8,128)(2,1)}, u32[]{:S(2)}, u32[]{:S(2)}) %collective-permute-start.1) | collective-permute-done | bytes 1572896 | tf_op jit(solution)/shard_map/ppermute | solution.py:16
  85.8 569.4 %while.71 = (s32[]{:T(128)}, bf16[512,1536]{1,0:T(8,128)(2,1)}, bf16[512,1536]{1,0:T(8,128)(2,1)}, s32[4]{0:T(128)S(1)}, s32[4]{0:T(128)S(1)}, /*index=5*/bf16[5...) while((s32[]{:T(128)}, bf16[512,1536]{1,0:T(8,128)(2,1)}, ...), condition=%wide.region_3.4_spmd, body=%wide.region_0.3_spmd.sunk | while | flops 12582925 | bytes 106955128 | solution.py:79
  92.3 68.2 %all-gather.11.cloned.1.call-done = bf16[4096,1536]{1,0:T(8,128)(2,1)} async-done(((bf16[128,1536]{1,0:T(8,128)(2,1)}), bf16[4096,1536]{1,0:T(8,128)(2,1)}) %all-gather.11.cloned.1.call-update) | async-done | bytes 12582928 | tf_op jit(solution)/shard_map/while/body/eval_jaxpr/all_gather | solution.py:21
  160.5 6.6 reduce_sum.61
  167.1 58.6 %all-gather.9.cloned.1.call-done = bf16[4096,1536]{1,0:T(8,128)(2,1)} async-done(((bf16[128,1536]{1,0:T(8,128)(2,1)}), bf16[4096,1536]{1,0:T(8,128)(2,1)}) %all-gather.9.cloned.1.call-update) | async-done | bytes 12582928 | tf_op jit(solution)/shard_map/while/body/eval_jaxpr/all_gather | solution.py:21
  225.7 6.6 reduce_sum.60
  240.4 60.6 %all-gather.11.cloned.1.call-done = bf16[4096,1536]{1,0:T(8,128)(2,1)} async-done(((bf16[128,1536]{1,0:T(8,128)(2,1)}), bf16[4096,1536]{1,0:T(8,128)(2,1)}) %all-gather.11.cloned.1.call-update) | async-done | bytes 12582928 | tf_op jit(solution)/shard_map/while/body/eval_jaxpr/all_gather | solution.py:21
  301.0 6.6 reduce_sum.61
  307.6 58.5 %all-gather.9.cloned.1.call-done = bf16[4096,1536]{1,0:T(8,128)(2,1)} async-done(((bf16[128,1536]{1,0:T(8,128)(2,1)}), bf16[4096,1536]{1,0:T(8,128)(2,1)}) %all-gather.9.cloned.1.call-update) | async-done | bytes 12582928 | tf_op jit(solution)/shard_map/while/body/eval_jaxpr/all_gather | solution.py:21
  366.1 6.6 reduce_sum.60
  380.8 60.6 %all-gather.11.cloned.1.call-done = bf16[4096,1536]{1,0:T(8,128)(2,1)} async-done(((bf16[128,1536]{1,0:T(8,128)(2,1)}), bf16[4096,1536]{1,0:T(8,128)(2,1)}) %all-gather.11.cloned.1.call-update) | async-done | bytes 12582928 | tf_op jit(solution)/shard_map/while/body/eval_jaxpr/all_gather | solution.py:21
  441.4 6.6 reduce_sum.61
  448.0 58.5 %all-gather.9.cloned.1.call-done = bf16[4096,1536]{1,0:T(8,128)(2,1)} async-done(((bf16[128,1536]{1,0:T(8,128)(2,1)}), bf16[4096,1536]{1,0:T(8,128)(2,1)}) %all-gather.9.cloned.1.call-update) | async-done | bytes 12582928 | tf_op jit(solution)/shard_map/while/body/eval_jaxpr/all_gather | solution.py:21
  521.2 60.6 %all-gather.11.cloned.1.call-done = bf16[4096,1536]{1,0:T(8,128)(2,1)} async-done(((bf16[128,1536]{1,0:T(8,128)(2,1)}), bf16[4096,1536]{1,0:T(8,128)(2,1)}) %all-gather.11.cloned.1.call-update) | async-done | bytes 12582928 | tf_op jit(solution)/shard_map/while/body/eval_jaxpr/all_gather | solution.py:21
  581.8 6.6 reduce_sum.61
  588.4 58.6 %all-gather.9.cloned.1.call-done = bf16[4096,1536]{1,0:T(8,128)(2,1)} async-done(((bf16[128,1536]{1,0:T(8,128)(2,1)}), bf16[4096,1536]{1,0:T(8,128)(2,1)}) %all-gather.9.cloned.1.call-update) | async-done | bytes 12582928 | tf_op jit(solution)/shard_map/while/body/eval_jaxpr/all_gather | solution.py:21
  674.6 162.4 %while.72 = (s32[]{:T(128)}, bf16[512,1536]{1,0:T(8,128)(2,1)}, f32[1024,1536]{1,0:T(8,128)}, f32[1024,1536]{1,0:T(8,128)}, f32[12,512]{1,0:T(8,128)S(1)}, /*ind...) while((s32[]{:T(128)}, bf16[512,1536]{1,0:T(8,128)(2,1)}, ...), condition=%wide.region_9.10_spmd, body=%wide.region_5.9_spmd.sunk | while | flops 1089731584 | bytes 42106048 | solution.py:143
  866.0 75.6 %while.73 = (s32[]{:T(128)}, f32[512,1536]{1,0:T(8,128)}, f32[512,1536]{1,0:T(8,128)}, bf16[512,1536]{1,0:T(8,128)(2,1)}, bf16[512,1536]{1,0:T(8,128)(2,1)}, /*i...) while((s32[]{:T(128)}, f32[512,1536]{1,0:T(8,128)}, ...), condition=%wide.region_12.13_spmd.clone, body=%wide.region_11.12_spmd.clone.sunk | while | flops 272039936 | bytes 5007079 | solution.py:187
  941.6 75.5 %while.74 = (s32[]{:T(128)}, f32[512,1536]{1,0:T(8,128)}, f32[512,1536]{1,0:T(8,128)}, bf16[512,1536]{1,0:T(8,128)(2,1)}, bf16[512,1536]{1,0:T(8,128)(2,1)}, /*i...) while((s32[]{:T(128)}, f32[512,1536]{1,0:T(8,128)}, ...), condition=%wide.region_14.15_spmd.clone, body=%wide.region_13.14_spmd.clone.sunk | while | flops 272039936 | bytes 5007079 | solution.py:187
  1017.1 10.6 scatter_custom_fusion.1
  1035.6 8.5 scatter_custom_fusion
  1045.4 10.5 all-to-all-done.2
  1066.5 12.4 %all-to-all-done.1 = bf16[4,128,1536]{2,1,0:T(8,128)(2,1)S(1)} async-done(((bf16[4,128,1536]{2,1,0:T(8,128)(2,1)}), bf16[4,128,1536]{2,1,0:T(8,128)(2,1)S(1)}, u32[]{:S(2)}, u32[]{:S(2)}) %all-to-all-start.1) | async-done | bytes 1572896 | tf_op jit(solution)/shard_map/all_to_all | solution.py:200
  (337 shorter events, 447.5 us)
Async XLA Ops:
  8.0 41.6 %collective-permute-start = (bf16[512,1536]{1,0:T(8,128)(2,1)}, bf16[512,1536]{1,0:T(8,128)(2,1)}, u32[]{:S(2)}, u32[]{:S(2)}) collective-permute-start(bf16[512,1536]{1,0:T(8,128)(2,1)} %param.14), channel_id=1, source_target_pairs={{0,8},{4,12},{8,16},{12,20},{16,24},{20,28},{24,32},{28,36},{32,40... | collective-permute-start | bytes 4718600 | tf_op jit(solution)/shard_map/ppermute | solution.py:16
  11.8 69.3 %collective-permute-start.1 = (bf16[512,1536]{1,0:T(8,128)(2,1)}, bf16[512,1536]{1,0:T(8,128)(2,1)}, u32[]{:S(2)}, u32[]{:S(2)}) collective-permute-start(bf16[512,1536]{1,0:T(8,128)(2,1)} %param.14), channel_id=1, source_target_pairs={{0,4},{4,8},{8,12},{12,16},{16,20},{20,24},{24,28},{28,32},{32,36}... | collective-permute-start | bytes 4718600 | tf_op jit(solution)/shard_map/ppermute | solution.py:16
  13.8 647.9 %collective-permute-start.2 = (bf16[512,1536]{1,0:T(8,128)(2,1)}, bf16[512,1536]{1,0:T(8,128)(2,1)}, u32[]{:S(2)}, u32[]{:S(2)}) collective-permute-start(bf16[512,1536]{1,0:T(8,128)(2,1)} %param.15), channel_id=1, source_target_pairs={{0,8},{4,12},{8,16},{12,20},{16,24},{20,28},{24,32},{28,36},{32,40... | collective-permute-start | bytes 4718600 | tf_op jit(solution)/shard_map/ppermute | solution.py:16
  17.6 644.1 %collective-permute-start.3 = (bf16[512,1536]{1,0:T(8,128)(2,1)}, bf16[512,1536]{1,0:T(8,128)(2,1)}, u32[]{:S(2)}, u32[]{:S(2)}) collective-permute-start(bf16[512,1536]{1,0:T(8,128)(2,1)} %param.15), channel_id=1, source_target_pairs={{0,4},{4,8},{8,12},{12,16},{16,20},{20,24},{24,28},{28,32},{32,36}... | collective-permute-start | bytes 4718600 | tf_op jit(solution)/shard_map/ppermute | solution.py:16
  21.0 839.7 %collective-permute-start.6 = (bf16[512,1536]{1,0:T(8,128)(2,1)}, bf16[512,1536]{1,0:T(8,128)(2,1)}, u32[]{:S(2)}, u32[]{:S(2)}) collective-permute-start(bf16[512,1536]{1,0:T(8,128)(2,1)} %param.16), channel_id=1, source_target_pairs={{4,0},{8,4},{12,8},{16,12},{20,16},{24,20},{28,24},{32,28},{36,32}... | collective-permute-start | bytes 4718600 | tf_op jit(solution)/shard_map/ppermute | solution.py:16
  49.6 892.0 %collective-permute-start.10 = (bf16[512,1536]{1,0:T(8,128)(2,1)}, bf16[512,1536]{1,0:T(8,128)(2,1)}, u32[]{:S(2)}, u32[]{:S(2)}) collective-permute-start(bf16[512,1536]{1,0:T(8,128)(2,1)} %param.16), channel_id=1, source_target_pairs={{8,0},{12,4},{16,8},{20,12},{24,16},{28,20},{32,24},{36,28},{40,32... | collective-permute-start | bytes 4718600 | tf_op jit(solution)/shard_map/ppermute | solution.py:16
  81.2 776.8 %collective-permute-start.4 = (bf16[512,1536]{1,0:T(8,128)(2,1)}, bf16[512,1536]{1,0:T(8,128)(2,1)}, u32[]{:S(2)}, u32[]{:S(2)}) collective-permute-start(bf16[512,1536]{1,0:T(8,128)(2,1)} %param.13), channel_id=1, source_target_pairs={{4,0},{8,4},{12,8},{16,12},{20,16},{24,20},{28,24},{32,28},{36,32}... | collective-permute-start | bytes 4718600 | tf_op jit(solution)/shard_map/ppermute | solution.py:16
  85.8 74.7 %all-gather.11.cloned.1.call-start = ((), (), s32[]{:S(2)}) async-start(), calls=%async_computation.5 | async-start | bytes 12976128 | tf_op jit(solution)/shard_map/while/body/eval_jaxpr/all_gather | solution.py:21
  90.3 135.4 %all-gather.9.cloned.1.call-start = ((), (), s32[]{:S(2)}) async-start(), calls=%async_computation.4 | async-start | bytes 12976128 | tf_op jit(solution)/shard_map/while/body/eval_jaxpr/all_gather | solution.py:21
  233.9 67.1 %all-gather.11.cloned.1.call-start = ((), (), s32[]{:S(2)}) async-start(), calls=%async_computation.5 | async-start | bytes 12976128 | tf_op jit(solution)/shard_map/while/body/eval_jaxpr/all_gather | solution.py:21
  238.5 127.7 %all-gather.9.cloned.1.call-start = ((), (), s32[]{:S(2)}) async-start(), calls=%async_computation.4 | async-start | bytes 12976128 | tf_op jit(solution)/shard_map/while/body/eval_jaxpr/all_gather | solution.py:21
  374.3 67.1 %all-gather.11.cloned.1.call-start = ((), (), s32[]{:S(2)}) async-start(), calls=%async_computation.5 | async-start | bytes 12976128 | tf_op jit(solution)/shard_map/while/body/eval_jaxpr/all_gather | solution.py:21
  378.8 127.7 %all-gather.9.cloned.1.call-start = ((), (), s32[]{:S(2)}) async-start(), calls=%async_computation.4 | async-start | bytes 12976128 | tf_op jit(solution)/shard_map/while/body/eval_jaxpr/all_gather | solution.py:21
  514.7 67.1 %all-gather.11.cloned.1.call-start = ((), (), s32[]{:S(2)}) async-start(), calls=%async_computation.5 | async-start | bytes 12976128 | tf_op jit(solution)/shard_map/while/body/eval_jaxpr/all_gather | solution.py:21
  519.2 127.8 %all-gather.9.cloned.1.call-start = ((), (), s32[]{:S(2)}) async-start(), calls=%async_computation.4 | async-start | bytes 12976128 | tf_op jit(solution)/shard_map/while/body/eval_jaxpr/all_gather | solution.py:21
  837.0 26.1 %collective-permute-start.5 = (f32[12,512]{1,0:T(8,128)S(1)}, f32[12,512]{1,0:T(8,128)S(1)}, u32[]{:S(2)}, u32[]{:S(2)}) collective-permute-start(f32[12,512]{1,0:T(8,128)S(1)} %get-tuple-element.734), channel_id=1, source_target_pairs={{4,0},{8,4},{12,8},{16,12},{20,16},{24,20},{28,24},{32,28},{36,32}... | collective-permute-start | bytes 73736 | tf_op jit(solution)/shard_map/ppermute | solution.py:16
  841.2 24.7 %collective-permute-start.7 = (f32[12,512]{1,0:T(8,128)S(1)}, f32[12,512]{1,0:T(8,128)S(1)}, u32[]{:S(2)}, u32[]{:S(2)}) collective-permute-start(f32[12,512]{1,0:T(8,128)S(1)} %get-tuple-element.735), channel_id=1, source_target_pairs={{4,0},{8,4},{12,8},{16,12},{20,16},{24,20},{28,24},{32,28},{36,32}... | collective-permute-start | bytes 73736 | tf_op jit(solution)/shard_map/ppermute | solution.py:16
  853.0 178.0 %all-to-all-start = ((bf16[4,128,1536]{2,1,0:T(8,128)(2,1)}), bf16[4,128,1536]{2,1,0:T(8,128)(2,1)}, u32[]{:S(2)}, u32[]{:S(2)}) async-start(bf16[4,128,1536]{2,1,0:T(8,128)(2,1)} %bitcast.8), calls=%async_computation | async-start | bytes 3145728 | tf_op jit(solution)/shard_map/all_to_all | solution.py:199
  857.4 159.7 %all-reduce.3.cloned.1.call-start = ((), (), s32[]{:S(2)}) async-start(), calls=%async_computation.3 | async-start | bytes 12582912 | tf_op jit(solution)/shard_map/psum | solution.py:195
  858.0 83.5 %collective-permute-start.8 = (bf16[512,1536]{1,0:T(8,128)(2,1)}, bf16[512,1536]{1,0:T(8,128)(2,1)}, u32[]{:S(2)}, u32[]{:S(2)}) collective-permute-start(bf16[512,1536]{1,0:T(8,128)(2,1)} %param.13), channel_id=1, source_target_pairs={{8,0},{12,4},{16,8},{20,12},{24,16},{28,20},{32,24},{36,28},{40,32... | collective-permute-start | bytes 4718600 | tf_op jit(solution)/shard_map/ppermute | solution.py:16
  860.7 80.8 %collective-permute-start.11 = (f32[12,512]{1,0:T(8,128)S(1)}, f32[12,512]{1,0:T(8,128)S(1)}, u32[]{:S(2)}, u32[]{:S(2)}) collective-permute-start(f32[12,512]{1,0:T(8,128)S(1)} %get-tuple-element.735), channel_id=1, source_target_pairs={{8,0},{12,4},{16,8},{20,12},{24,16},{28,20},{32,24},{36,28},{40,32... | collective-permute-start | bytes 73736 | tf_op jit(solution)/shard_map/ppermute | solution.py:16
  863.1 78.5 %collective-permute-start.9 = (f32[12,512]{1,0:T(8,128)S(1)}, f32[12,512]{1,0:T(8,128)S(1)}, u32[]{:S(2)}, u32[]{:S(2)}) collective-permute-start(f32[12,512]{1,0:T(8,128)S(1)} %get-tuple-element.734), channel_id=1, source_target_pairs={{8,0},{12,4},{16,8},{20,12},{24,16},{28,20},{32,24},{36,28},{40,32... | collective-permute-start | bytes 73736 | tf_op jit(solution)/shard_map/ppermute | solution.py:16
  1031.1 24.9 %all-to-all-start.2 = ((bf16[4,128,1536]{2,1,0:T(8,128)(2,1)}), bf16[4,128,1536]{2,1,0:T(8,128)(2,1)}, u32[]{:S(2)}, u32[]{:S(2)}) async-start(bf16[4,128,1536]{2,1,0:T(8,128)(2,1)} %bitcast.74), calls=%async_computation.2 | async-start | bytes 3145728 | tf_op jit(solution)/shard_map/all_to_all | solution.py:201
  1056.0 22.9 %all-to-all-start.1 = ((bf16[4,128,1536]{2,1,0:T(8,128)(2,1)}), bf16[4,128,1536]{2,1,0:T(8,128)(2,1)S(1)}, u32[]{:S(2)}, u32[]{:S(2)}) async-start(bf16[4,128,1536]{2,1,0:T(8,128)(2,1)} %bitcast.75), calls=%async_computation.1 | async-start | bytes 3145728 | tf_op jit(solution)/shard_map/all_to_all | solution.py:200
  (4 other events, 79.2 us)
Sparse Core Ops, SparseCore 0:
  90.5 69.9 all-gather.10
  163.3 62.3 all-gather.8
  238.6 62.3 all-gather.10
  303.7 62.3 all-gather.8
  379.0 62.3 all-gather.10
  444.1 62.3 all-gather.8
  519.3 62.3 all-gather.10
  584.6 62.3 all-gather.8
Sparse Core Ops, SparseCore 1:
  861.4 130.8 all-reduce.2
